TPU v7x, 32 devices: a whole 2x2x4 slice. The times are simulated.
32 devices in a mesh: wide: 8 (over z, y), narrow: 4 (over x, core).
Axes of the slice: x: 2, y: 2, z: 4, core: 2. Of those that a mesh axis runs over, the one named last changes fastest.
Arguments:
- right_side: float32 [112, 224, 256], P('narrow', 'wide'), may hold values from -60 to 60
- initial_guess: float32 [112, 224, 256], P('narrow', 'wide'), may hold values from -6 to 6
- class_map: int32 [112, 224], P('narrow', 'wide'), may hold values from 0 to 7
- class_conductivity: float32 [8], replicated, may hold values from 0.2 to 2
- window_index: int32 [4, 8, 1024], P('narrow', 'wide'), may hold values from 0 to 1023, each once within a row
- local_inverse: float32 [4, 8, 1024, 1024], P('narrow', 'wide'), may hold values from -1 to 1
- coarse_basis: float32 [4, 8, 4, 1024], P('narrow', 'wide'), may hold values from -0.1875 to 0.1875
- coarse_inverse: float32 [128, 128], P('wide', 'narrow'), may hold values from -8 to 8
Outputs:
- solution: float32 [112, 224, 256], P('narrow', 'wide')
- residual: float32 [112, 224, 256], P('narrow', 'wide')
All inputs are finite; a program needn't handle non-finite values.
Results may differ from a plain program's by a relative error of at most 0.00013.
Values sent between devices are 32-bit elements; how exact they have to be, the bound alone decides.
A program may use at most 64 MiB of HBM per device.

v0:
```python
import jax
import jax.numpy as jnp
from jax import lax
from jax.sharding import PartitionSpec as P

ES = 32
OV = 2
MODES = 4
ITERS = 3
CS = 28
LOCAL = 1024


HIGHEST = lax.Precision.HIGHEST
REACTION = 0.01
NEIGHBOURS = ((0, 1), (2, 1), (1, 0), (1, 2))


def extended_2(cells, sides, width):
    for axis, dim in sides:
        count = lax.axis_size(axis)
        ends = count - 1
        head = lax.slice_in_dim(cells, 0, width, axis=dim)
        tail = lax.slice_in_dim(cells, cells.shape[dim] - width, cells.shape[dim], axis=dim)
        cells = jnp.concatenate(
            [
                lax.ppermute(tail, axis, [(i, (i + 1) % count) for i in range(ends)]),
                cells,
                lax.ppermute(head, axis, [((i + 1) % count, i) for i in range(ends)]),
            ],
            axis=dim,
        )
    return cells


def apply_operator(padded_field, conduct):
    height = padded_field.shape[0] - 2
    breadth = padded_field.shape[1] - 2
    centre = padded_field[1 : height + 1, 1 : breadth + 1]
    own_conduct = conduct[1 : height + 1, 1 : breadth + 1]
    result = REACTION * centre
    for row_shift, col_shift in NEIGHBOURS:
        beside = padded_field[row_shift : row_shift + height, col_shift : col_shift + breadth]
        face_weight = 0.5 * (
            own_conduct + conduct[row_shift : row_shift + height, col_shift : col_shift + breadth]
        )
        result = result + face_weight[:, :, None] * (centre - beside)
    return result


def local(
    right_side,
    initial_guess,
    class_map,
    class_conductivity,
    window_index,
    local_inverse,
    coarse_basis,
    coarse_inverse,
):
    classes = class_conductivity.shape[0]
    columns = right_side.shape[2]
    matches = class_map[:, :, None] == jnp.arange(classes, dtype=jnp.int32)[None, None, :]
    conduct = jnp.sum(jnp.where(matches, class_conductivity[None, None, :], 0.0), axis=2)
    local_order = window_index[0, 0]
    inverse_order = jnp.argsort(local_order)
    inverse_local = local_inverse[0, 0]
    mode_basis = coarse_basis[0, 0]
    tile_view = coarse_inverse.reshape(
        coarse_inverse.shape[0], coarse_inverse.shape[1] // MODES, MODES
    )
    guess_ext = extended_2(initial_guess, (("wide", 1), ("narrow", 0)), 1)
    solution = initial_guess
    conduct_deep = extended_2(conduct, (("wide", 1), ("narrow", 0)), OV + 1)
    conduct_near = conduct_deep[OV : OV + CS + 2, OV : OV + CS + 2]
    residual_first = right_side - apply_operator(guess_ext, conduct_near)
    residual_window = extended_2(residual_first, (("wide", 1), ("narrow", 0)), OV)
    row_pos = lax.axis_index("narrow") * CS - OV + jnp.arange(ES, dtype=jnp.int32)
    col_pos = lax.axis_index("wide") * CS - OV + jnp.arange(ES, dtype=jnp.int32)
    row_inside = (row_pos >= 0) & (row_pos < CS * lax.axis_size("narrow"))
    col_inside = (col_pos >= 0) & (col_pos < CS * lax.axis_size("wide"))
    inside_mask = (row_inside[:, None] & col_inside[None, :]).astype(jnp.float32)[:, :, None]
    for iteration in range(ITERS):
        gathered = residual_window.reshape(LOCAL, columns)[local_order]
        local_part = jnp.dot(
            inverse_local, gathered, precision=HIGHEST, preferred_element_type=jnp.float32
        )
        coarse_rhs = jnp.dot(
            mode_basis, gathered, precision=HIGHEST, preferred_element_type=jnp.float32
        )
        partial_rows = jnp.einsum(
            "ibm,bmr->ir",
            tile_view,
            lax.all_gather(coarse_rhs[None], "wide", axis=0, tiled=True),
            precision=HIGHEST,
            preferred_element_type=jnp.float32,
        )
        coarse_sol = lax.psum_scatter(partial_rows, "narrow", scatter_dimension=0, tiled=True)
        extended = local_part + jnp.einsum(
            "mk,mr->kr",
            mode_basis,
            coarse_sol,
            precision=HIGHEST,
            preferred_element_type=jnp.float32,
        )
        windowed = extended[inverse_order].reshape(ES, ES, columns)
        direction = windowed[OV : OV + CS, OV : OV + CS]
        direction_deep = extended_2(direction, (("wide", 1), ("narrow", 0)), OV + 1)
        image_window = apply_operator(direction_deep, conduct_deep) * inside_mask
        image = image_window[OV : OV + CS, OV : OV + CS]
        numer, denom = lax.psum(
            (
                jnp.sum(residual_window[OV : OV + CS, OV : OV + CS] * image, axis=(0, 1)),
                jnp.sum(image * image, axis=(0, 1)),
            ),
            ("wide", "narrow"),
        )
        stepsize = numer / denom
        solution = solution + stepsize * direction
        residual_window = residual_window - stepsize * image_window
    return (solution, residual_window[OV : OV + CS, OV : OV + CS])


def solution(mesh):
    in_specs = (
        P("narrow", "wide", None),
        P("narrow", "wide", None),
        P("narrow", "wide"),
        P(),
        P("narrow", "wide", None),
        P("narrow", "wide", None, None),
        P("narrow", "wide", None, None),
        P("wide", "narrow"),
    )
    out_specs = (P("narrow", "wide", None), P("narrow", "wide", None))
    return jax.shard_map(local, mesh=mesh, in_specs=in_specs, out_specs=out_specs, check_vma=False)
```

profile of v0, /device:TPU:1, one launch (start us, length us, event | category | flops | bytes accessed | tf_op | source)
XLA Modules:
  0.0 426.2 jit_solution(5896631646058983150)
XLA Ops:
  1.7 4.0 collective-permute-start
  8.0 4.0 collective-permute-start.3
  14.2 4.5 %collective-permute-start.2 = (f32[3,34]{1,0:T(4,128)S(1)}, f32[3,34]{1,0:T(4,128)S(1)}, u32[]{:S(2)}, u32[]{:S(2)}) collective-permute-start(f32[3,34]{1,0:T(4,128)S(1)} %get-tuple-element.38), channel_id=1, source_target_pairs={{0,1},{1,2},{2,3},{4,5},{5,6},{6,7},{8,9},{9,10},{10,11},{12,13},{... | collective-permute-start | bytes 1232 | tf_op jit(solution)/shard_map/ppermute | solution.py:27
  21.5 3.6 collective-permute-start.5
  33.0 4.7 %collective-permute-start.8 = (f32[28,2,256]{2,1,0:T(2,128)S(1)}, f32[28,2,256]{2,1,0:T(2,128)S(1)}, u32[]{:S(2)}, u32[]{:S(2)}) collective-permute-start(f32[28,2,256]{2,1,0:T(2,128)S(1)} %get-tuple-element.32), channel_id=1, source_target_pairs={{0,4},{4,8},{8,12},{12,16},{16,20},{20,24},{24,28},{1,5},{5,9},{9,... | collective-permute-start | bytes 172040 | tf_op jit(solution)/shard_map/ppermute | solution.py:27
  39.0 4.4 %sort.17 = (s32[1024]{0:T(1024)}, s32[1024]{0:T(1024)S(1)}) sort(s32[1024]{0:T(1024)S(1)} %bitcast.107, s32[1024]{0:T(1024)S(1)} %iota.18), dimensions={0}, to_apply=%region_2.3 | sort | flops 10240 | bytes 16384 | tf_op jit(solution)/shard_map/jit(argsort)/sort | solution.py:66
  53.1 3.5 gather_fusion
  57.2 26.7 %all-gather.3 = f32[8,4,256]{2,1,0:T(4,128)S(1)} all-gather(f32[1,4,256]{2,1,0:T(4,128)S(1)} %convolution_bitcast_fusion.5), channel_id=2, replica_groups=mesh['wide'=8,'narrow'=4] {'wide'}, dimensions={0}, use_global_device_ids=true | all-gather | bytes 36864 | tf_op jit(solution)/shard_map/all_gather | solution.py:94
  84.2 16.4 %all-reduce = f32[16,256]{0,1:T(8,128)S(1)} all-reduce(f32[16,256]{0,1:T(8,128)S(1)} %copy.25), channel_id=5, replica_groups=mesh['wide'=8,'narrow'=4] {'narrow'}, use_global_device_ids=true, to_apply=%region_1.2.clone | all-reduce | flops 4096 | bytes 32768
  101.7 10.0 %fusion.9 = f32[1024,256]{0,1:T(8,128)} fusion(f32[256,1024]{1,0:T(8,128)S(1)} %fusion.69, f32[1024,256]{1,0:T(8,128)S(1)} %gather_fusion, f32[1,1,1024,1024]{3,2,1,0:T(8,128)} %param.13), kind=kOutput, calls=%fused_computation.16 | convolution fusion | flops 3221487616 | bytes 7340032 | tf_op jit(solution)/shard_map/dot_general | solution.py:85
  113.3 3.5 gather_fusion.1
  121.1 3.9 collective-permute-done.13
  125.0 3.5 collective-permute-start.14
  130.6 4.2 collective-permute-done.15
  136.3 38.0 %all-reduce.5 = (f32[256]{0:T(256)S(1)}, f32[256]{0:T(256)S(1)}) all-reduce(f32[256]{0:T(256)S(1)} %get-tuple-element.9, f32[256]{0:T(256)S(1)} %get-tuple-element.8), channel_id=1, replica_groups=mesh['wide'=8,'narrow'=4] {'wide','narrow'}, use_global_device_ids=true, to_apply=%region_4.5 | all-reduce | flops 512 | bytes 4096 | tf_op jit(solution)/shard_map/psum | solution.py:111
  176.7 3.5 gather_fusion.2
  180.8 24.5 %all-gather.4 = f32[8,4,256]{2,1,0:T(4,128)S(1)} all-gather(f32[1,4,256]{2,1,0:T(4,128)S(1)} %convolution_bitcast_fusion.4), channel_id=3, replica_groups=mesh['wide'=8,'narrow'=4] {'wide'}, dimensions={0}, use_global_device_ids=true | all-gather | bytes 36864 | tf_op jit(solution)/shard_map/all_gather | solution.py:94
  205.5 19.7 %all-reduce.1 = f32[16,256]{0,1:T(8,128)S(1)} all-reduce(f32[16,256]{0,1:T(8,128)S(1)} %copy.27), channel_id=6, replica_groups=mesh['wide'=8,'narrow'=4] {'narrow'}, use_global_device_ids=true, to_apply=%region_7.8.clone | all-reduce | flops 4096 | bytes 32768
  226.2 8.7 %fusion.15 = f32[1024,256]{0,1:T(8,128)S(1)} fusion(f32[256,1024]{1,0:T(8,128)S(1)} %fusion.67, f32[1024,256]{1,0:T(8,128)S(1)} %gather_fusion.2, f32[1,1,1024,1024]{3,2,1,0:T(8,128)} %param.13), kind=kOutput, calls=%fused_computation.18 | convolution fusion | flops 3221487616 | bytes 7340032 | tf_op jit(solution)/shard_map/dot_general | solution.py:85
  242.5 3.8 collective-permute-done.17
  246.4 4.5 %collective-permute-start.18 = (f32[3,34,256]{2,1,0:T(8,128)S(1)}, f32[3,34,256]{2,1,0:T(8,128)S(1)}, u32[]{:S(2)}, u32[]{:S(2)}) collective-permute-start(f32[3,34,256]{2,1,0:T(8,128)S(1)} %get-tuple-element.18), channel_id=1, source_target_pairs={{0,1},{1,2},{2,3},{4,5},{5,6},{6,7},{8,9},{9,10},{10,11},{12,13},{... | collective-permute-start | bytes 313352 | tf_op jit(solution)/shard_map/ppermute | solution.py:27
  252.9 4.3 collective-permute-done.19
  259.4 38.2 %all-reduce.4 = (f32[256]{0:T(256)S(1)}, f32[256]{0:T(256)S(1)}) all-reduce(f32[256]{0:T(256)} %get-tuple-element.7, f32[256]{0:T(256)} %get-tuple-element.6), channel_id=1, replica_groups=mesh['wide'=8,'narrow'=4] {'wide','narrow'}, use_global_device_ids=true, to_apply=%region_9.10 | all-reduce | flops 512 | bytes 4096 | tf_op jit(solution)/shard_map/psum | solution.py:111
  299.5 4.0 gather_fusion.4
  304.1 24.2 %all-gather.5 = f32[8,4,256]{2,1,0:T(4,128)S(1)} all-gather(f32[1,4,256]{2,1,0:T(4,128)S(1)} %convolution_bitcast_fusion.3), channel_id=4, replica_groups=mesh['wide'=8,'narrow'=4] {'wide'}, dimensions={0}, use_global_device_ids=true | all-gather | bytes 36864 | tf_op jit(solution)/shard_map/all_gather | solution.py:94
  328.7 19.9 %all-reduce.2 = f32[16,256]{0,1:T(8,128)S(1)} all-reduce(f32[16,256]{0,1:T(8,128)S(1)} %copy.29), channel_id=7, replica_groups=mesh['wide'=8,'narrow'=4] {'narrow'}, use_global_device_ids=true, to_apply=%region_12.13.clone | all-reduce | flops 4096 | bytes 32768
  349.6 8.7 %fusion.21 = f32[1024,256]{0,1:T(8,128)S(1)} fusion(f32[256,1024]{1,0:T(8,128)S(1)} %fusion.65, f32[1024,256]{1,0:T(8,128)S(1)} %gather_fusion.4, f32[1,1,1024,1024]{3,2,1,0:T(8,128)} %param.13), kind=kOutput, calls=%fused_computation.20 | convolution fusion | flops 3221487616 | bytes 7340032 | tf_op jit(solution)/shard_map/dot_general | solution.py:85
  366.0 3.8 collective-permute-done.21
  369.8 4.5 %collective-permute-start.22 = (f32[3,34,256]{2,1,0:T(8,128)S(1)}, f32[3,34,256]{2,1,0:T(8,128)S(1)}, u32[]{:S(2)}, u32[]{:S(2)}) collective-permute-start(f32[3,34,256]{2,1,0:T(8,128)S(1)} %get-tuple-element.16), channel_id=1, source_target_pairs={{0,1},{1,2},{2,3},{4,5},{5,6},{6,7},{8,9},{9,10},{10,11},{12,13},{... | collective-permute-start | bytes 313352 | tf_op jit(solution)/shard_map/ppermute | solution.py:27
  376.3 4.3 collective-permute-done.23
  384.3 38.0 %all-reduce.3 = (f32[256]{0:T(256)S(1)}, f32[256]{0:T(256)S(1)}) all-reduce(f32[256]{0:T(256)S(1)} %get-tuple-element.5, f32[256]{0:T(256)S(1)} %get-tuple-element.4), channel_id=1, replica_groups=mesh['wide'=8,'narrow'=4] {'wide','narrow'}, use_global_device_ids=true, to_apply=%region_14.15 | all-reduce | flops 512 | bytes 4096 | tf_op jit(solution)/shard_map/psum | solution.py:111
  422.3 3.8 multiply_subtract_fusion.2
  (152 shorter events, 71.0 us)
Async XLA Ops:
  0.6 55.9 %copy-start = (f32[1,1,4,1024]{3,2,1,0:T(4,128)S(1)}, f32[1,1,4,1024]{3,2,1,0:T(4,128)}, u32[]{:S(2)}) copy-start(f32[1,1,4,1024]{3,2,1,0:T(4,128)} %param.14) | copy-start | bytes 49156
  1.7 12.4 %collective-permute-start = (f32[28,3]{1,0:T(8,128)S(1)}, f32[28,3]{1,0:T(8,128)S(1)}, u32[]{:S(2)}, u32[]{:S(2)}) collective-permute-start(f32[28,3]{1,0:T(8,128)S(1)} %get-tuple-element.46), channel_id=1, source_target_pairs={{0,4},{4,8},{8,12},{12,16},{16,20},{20,24},{24,28},{1,5},{5,9},{9,... | collective-permute-start | bytes 1016 | tf_op jit(solution)/shard_map/ppermute | solution.py:27
  5.6 8.5 %collective-permute-start.1 = (f32[28,3]{1,0:T(8,128)S(1)}, f32[28,3]{1,0:T(8,128)S(1)}, u32[]{:S(2)}, u32[]{:S(2)}) collective-permute-start(f32[28,3]{1,0:T(8,128)S(1)} %get-tuple-element.47), channel_id=1, source_target_pairs={{4,0},{8,4},{12,8},{16,12},{20,16},{24,20},{28,24},{5,1},{9,5},{13... | collective-permute-start | bytes 1016 | tf_op jit(solution)/shard_map/ppermute | solution.py:29
  8.0 12.6 %collective-permute-start.3 = (f32[28,1,256]{2,1,0:T(1,128)S(1)}, f32[28,1,256]{2,1,0:T(1,128)S(1)}, u32[]{:S(2)}, u32[]{:S(2)}) collective-permute-start(f32[28,1,256]{2,1,0:T(1,128)S(1)} %get-tuple-element.34), channel_id=1, source_target_pairs={{0,4},{4,8},{8,12},{12,16},{16,20},{20,24},{24,28},{1,5},{5,9},{9,... | collective-permute-start | bytes 86024 | tf_op jit(solution)/shard_map/ppermute | solution.py:27
  12.0 8.6 %collective-permute-start.4 = (f32[28,1,256]{2,1,0:T(1,128)S(1)}, f32[28,1,256]{2,1,0:T(1,128)S(1)}, u32[]{:S(2)}, u32[]{:S(2)}) collective-permute-start(f32[28,1,256]{2,1,0:T(1,128)S(1)} %get-tuple-element.35), channel_id=1, source_target_pairs={{4,0},{8,4},{12,8},{16,12},{20,16},{24,20},{28,24},{5,1},{9,5},{13... | collective-permute-start | bytes 86024 | tf_op jit(solution)/shard_map/ppermute | solution.py:29
  14.2 12.8 %collective-permute-start.2 = (f32[3,34]{1,0:T(4,128)S(1)}, f32[3,34]{1,0:T(4,128)S(1)}, u32[]{:S(2)}, u32[]{:S(2)}) collective-permute-start(f32[3,34]{1,0:T(4,128)S(1)} %get-tuple-element.38), channel_id=1, source_target_pairs={{0,1},{1,2},{2,3},{4,5},{5,6},{6,7},{8,9},{9,10},{10,11},{12,13},{... | collective-permute-start | bytes 1232 | tf_op jit(solution)/shard_map/ppermute | solution.py:27
  18.7 8.3 %collective-permute-start.6 = (f32[3,34]{1,0:T(4,128)S(1)}, f32[3,34]{1,0:T(4,128)S(1)}, u32[]{:S(2)}, u32[]{:S(2)}) collective-permute-start(f32[3,34]{1,0:T(4,128)S(1)} %get-tuple-element.39), channel_id=1, source_target_pairs={{1,0},{2,1},{3,2},{5,4},{6,5},{7,6},{9,8},{10,9},{11,10},{13,12},{... | collective-permute-start | bytes 1232 | tf_op jit(solution)/shard_map/ppermute | solution.py:29
  21.5 5.7 %collective-permute-start.5 = (f32[1,30,256]{2,1,0:T(8,128)S(1)}, f32[1,30,256]{2,1,0:T(8,128)S(1)}, u32[]{:S(2)}, u32[]{:S(2)}) collective-permute-start(f32[1,30,256]{2,1,0:T(8,128)S(1)} %get-tuple-element.30), channel_id=1, source_target_pairs={{0,1},{1,2},{2,3},{4,5},{5,6},{6,7},{8,9},{9,10},{10,11},{12,13},{... | collective-permute-start | bytes 92168 | tf_op jit(solution)/shard_map/ppermute | solution.py:27
  25.1 5.2 %collective-permute-start.7 = (f32[1,30,256]{2,1,0:T(8,128)S(1)}, f32[1,30,256]{2,1,0:T(8,128)S(1)}, u32[]{:S(2)}, u32[]{:S(2)}) collective-permute-start(f32[1,30,256]{2,1,0:T(8,128)S(1)} %get-tuple-element.31), channel_id=1, source_target_pairs={{1,0},{2,1},{3,2},{5,4},{6,5},{7,6},{9,8},{10,9},{11,10},{13,12},{... | collective-permute-start | bytes 92168 | tf_op jit(solution)/shard_map/ppermute | solution.py:29
  33.0 10.4 %collective-permute-start.8 = (f32[28,2,256]{2,1,0:T(2,128)S(1)}, f32[28,2,256]{2,1,0:T(2,128)S(1)}, u32[]{:S(2)}, u32[]{:S(2)}) collective-permute-start(f32[28,2,256]{2,1,0:T(2,128)S(1)} %get-tuple-element.32), channel_id=1, source_target_pairs={{0,4},{4,8},{8,12},{12,16},{16,20},{20,24},{24,28},{1,5},{5,9},{9,... | collective-permute-start | bytes 172040 | tf_op jit(solution)/shard_map/ppermute | solution.py:27
  37.7 6.1 %collective-permute-start.9 = (f32[28,2,256]{2,1,0:T(2,128)S(1)}, f32[28,2,256]{2,1,0:T(2,128)S(1)}, u32[]{:S(2)}, u32[]{:S(2)}) collective-permute-start(f32[28,2,256]{2,1,0:T(2,128)S(1)} %get-tuple-element.33), channel_id=1, source_target_pairs={{4,0},{8,4},{12,8},{16,12},{20,16},{24,20},{28,24},{5,1},{9,5},{13... | collective-permute-start | bytes 172040 | tf_op jit(solution)/shard_map/ppermute | solution.py:29
  39.0 137.7 %copy-start.18 = (s32[1024]{0:T(1024)}, s32[1024]{0:T(1024)S(1)}, u32[]{:S(2)}) copy-start(s32[1024]{0:T(1024)S(1)} %broadcast_clamp_fusion) | copy-start | bytes 12292
  43.8 6.4 %collective-permute-start.10 = (f32[2,32,256]{2,1,0:T(8,128)S(1)}, f32[2,32,256]{2,1,0:T(8,128)S(1)}, u32[]{:S(2)}, u32[]{:S(2)}) collective-permute-start(f32[2,32,256]{2,1,0:T(8,128)S(1)} %get-tuple-element.28), channel_id=1, source_target_pairs={{0,1},{1,2},{2,3},{4,5},{5,6},{6,7},{8,9},{9,10},{10,11},{12,13},{... | collective-permute-start | bytes 196616 | tf_op jit(solution)/shard_map/ppermute | solution.py:27
  46.9 5.6 %collective-permute-start.11 = (f32[2,32,256]{2,1,0:T(8,128)S(1)}, f32[2,32,256]{2,1,0:T(8,128)S(1)}, u32[]{:S(2)}, u32[]{:S(2)}) collective-permute-start(f32[2,32,256]{2,1,0:T(8,128)S(1)} %get-tuple-element.29), channel_id=1, source_target_pairs={{1,0},{2,1},{3,2},{5,4},{6,5},{7,6},{9,8},{10,9},{11,10},{13,12},{... | collective-permute-start | bytes 196616 | tf_op jit(solution)/shard_map/ppermute | solution.py:29
  48.8 64.5 %copy-start.19 = (s32[1024]{0:T(1024)}, s32[1024]{0:T(1024)S(1)}, u32[]{:S(2)}) copy-start(s32[1024]{0:T(1024)S(1)} %fusion.89) | copy-start | bytes 12292
  48.9 156.3 %copy-start.16 = (f32[16,32]{0,1:T(8,128)}, f32[16,32]{0,1:T(8,128)S(1)}, u32[]{:S(2)}) copy-start(f32[16,32]{0,1:T(8,128)S(1)} %copy.24) | copy-start | bytes 6148
  116.8 4.2 collective-permute-start.12
  118.1 6.8 %collective-permute-start.13 = (f32[28,3,256]{2,1,0:T(4,128)S(1)}, f32[28,3,256]{2,1,0:T(4,128)S(1)}, u32[]{:S(2)}, u32[]{:S(2)}) collective-permute-start(f32[28,3,256]{2,1,0:T(4,128)S(1)} %get-tuple-element.27), channel_id=1, source_target_pairs={{4,0},{8,4},{12,8},{16,12},{20,16},{24,20},{28,24},{5,1},{9,5},{13... | collective-permute-start | bytes 258056 | tf_op jit(solution)/shard_map/ppermute | solution.py:29
  125.0 5.6 %collective-permute-start.14 = (f32[3,34,256]{2,1,0:T(8,128)S(1)}, f32[3,34,256]{2,1,0:T(8,128)S(1)}, u32[]{:S(2)}, u32[]{:S(2)}) collective-permute-start(f32[3,34,256]{2,1,0:T(8,128)S(1)} %get-tuple-element.20), channel_id=1, source_target_pairs={{0,1},{1,2},{2,3},{4,5},{5,6},{6,7},{8,9},{9,10},{10,11},{12,13},{... | collective-permute-start | bytes 313352 | tf_op jit(solution)/shard_map/ppermute | solution.py:27
  128.5 6.2 %collective-permute-start.15 = (f32[3,34,256]{2,1,0:T(8,128)S(1)}, f32[3,34,256]{2,1,0:T(8,128)S(1)}, u32[]{:S(2)}, u32[]{:S(2)}) collective-permute-start(f32[3,34,256]{2,1,0:T(8,128)S(1)} %get-tuple-element.21), channel_id=1, source_target_pairs={{1,0},{2,1},{3,2},{5,4},{6,5},{7,6},{9,8},{10,9},{11,10},{13,12},{... | collective-permute-start | bytes 313352 | tf_op jit(solution)/shard_map/ppermute | solution.py:29
  130.6 43.8 %copy-start.7 = (f32[32,32]{1,0:T(8,128)}, f32[32,32]{1,0:T(8,128)S(1)}, u32[]{:S(2)}) copy-start(f32[32,32]{1,0:T(8,128)S(1)} %get-tuple-element.44) | copy-start | bytes 12292
  130.6 43.7 %copy-start.10 = (f32[32,32]{1,0:T(8,128)}, f32[32,32]{1,0:T(8,128)S(1)}, u32[]{:S(2)}) copy-start(f32[32,32]{1,0:T(8,128)S(1)} %get-tuple-element.45) | copy-start | bytes 12292
  239.1 3.4 collective-permute-start.16
  240.8 5.5 %collective-permute-start.17 = (f32[28,3,256]{2,1,0:T(4,128)S(1)}, f32[28,3,256]{2,1,0:T(4,128)S(1)}, u32[]{:S(2)}, u32[]{:S(2)}) collective-permute-start(f32[28,3,256]{2,1,0:T(4,128)S(1)} %get-tuple-element.25), channel_id=1, source_target_pairs={{4,0},{8,4},{12,8},{16,12},{20,16},{24,20},{28,24},{5,1},{9,5},{13... | collective-permute-start | bytes 258056 | tf_op jit(solution)/shard_map/ppermute | solution.py:29
  246.4 6.6 %collective-permute-start.18 = (f32[3,34,256]{2,1,0:T(8,128)S(1)}, f32[3,34,256]{2,1,0:T(8,128)S(1)}, u32[]{:S(2)}, u32[]{:S(2)}) collective-permute-start(f32[3,34,256]{2,1,0:T(8,128)S(1)} %get-tuple-element.18), channel_id=1, source_target_pairs={{0,1},{1,2},{2,3},{4,5},{5,6},{6,7},{8,9},{9,10},{10,11},{12,13},{... | collective-permute-start | bytes 313352 | tf_op jit(solution)/shard_map/ppermute | solution.py:27
  250.9 6.3 %collective-permute-start.19 = (f32[3,34,256]{2,1,0:T(8,128)S(1)}, f32[3,34,256]{2,1,0:T(8,128)S(1)}, u32[]{:S(2)}, u32[]{:S(2)}) collective-permute-start(f32[3,34,256]{2,1,0:T(8,128)S(1)} %get-tuple-element.19), channel_id=1, source_target_pairs={{1,0},{2,1},{3,2},{5,4},{6,5},{7,6},{9,8},{10,9},{11,10},{13,12},{... | collective-permute-start | bytes 313352 | tf_op jit(solution)/shard_map/ppermute | solution.py:29
  362.5 3.4 collective-permute-start.20
  364.2 5.5 %collective-permute-start.21 = (f32[28,3,256]{2,1,0:T(4,128)S(1)}, f32[28,3,256]{2,1,0:T(4,128)S(1)}, u32[]{:S(2)}, u32[]{:S(2)}) collective-permute-start(f32[28,3,256]{2,1,0:T(4,128)S(1)} %get-tuple-element.23), channel_id=1, source_target_pairs={{4,0},{8,4},{12,8},{16,12},{20,16},{24,20},{28,24},{5,1},{9,5},{13... | collective-permute-start | bytes 258056 | tf_op jit(solution)/shard_map/ppermute | solution.py:29
  369.8 6.6 %collective-permute-start.22 = (f32[3,34,256]{2,1,0:T(8,128)S(1)}, f32[3,34,256]{2,1,0:T(8,128)S(1)}, u32[]{:S(2)}, u32[]{:S(2)}) collective-permute-start(f32[3,34,256]{2,1,0:T(8,128)S(1)} %get-tuple-element.16), channel_id=1, source_target_pairs={{0,1},{1,2},{2,3},{4,5},{5,6},{6,7},{8,9},{9,10},{10,11},{12,13},{... | collective-permute-start | bytes 313352 | tf_op jit(solution)/shard_map/ppermute | solution.py:27
  374.3 6.3 %collective-permute-start.23 = (f32[3,34,256]{2,1,0:T(8,128)S(1)}, f32[3,34,256]{2,1,0:T(8,128)S(1)}, u32[]{:S(2)}, u32[]{:S(2)}) collective-permute-start(f32[3,34,256]{2,1,0:T(8,128)S(1)} %get-tuple-element.17), channel_id=1, source_target_pairs={{1,0},{2,1},{3,2},{5,4},{6,5},{7,6},{9,8},{10,9},{11,10},{13,12},{... | collective-permute-start | bytes 313352 | tf_op jit(solution)/shard_map/ppermute | solution.py:29
  380.8 41.5 %copy-start.4 = (f32[1024,256]{1,0:T(8,128)S(1)}, f32[1024,256]{1,0:T(8,128)}, u32[]{:S(2)}) copy-start(f32[1024,256]{1,0:T(8,128)} %copy-done.3) | copy-start | bytes 3145732
  382.8 39.5 %copy-start.26 = (f32[256]{0:T(256)S(1)}, f32[256]{0:T(256)}, u32[]{:S(2)}) copy-start(f32[256]{0:T(256)} %copy-done.25) | copy-start | bytes 3076
  (21 other events, 255.4 us)
where the time goes:
time: 429 us; the launch traced here: 426 us
  blocking collectives  246 us (57%)
  starting transfers between devices  60.4 us (14%)
  matrix products  33 us (8%)
  waiting for transfers between devices  32.1 us (7%)
  local copies, waits for them, and re-layouts  27.3 us (6%)
  other arithmetic  25.5 us (6%)
    psum x3, blocking collectives, local(): lax.psum((jnp.sum(residual_window[OV:OV + CS, OV:OV + CS] * image, axis=(...  114 us
    all_gather x3, blocking collectives, local(): lax.all_gather(coarse_rhs[None], 'wide', axis=0, tiled=True)  75.4 us
    unnamed x3, blocking collectives  56 us
    ppermute x12, starting transfers between devices, extended_2(): lax.ppermute(tail, axis, [(i, (i + 1) % count) for i in range(ends)])  40.9 us
    ppermute x12, waiting for transfers between devices, extended_2(): lax.ppermute(head, axis, [((i + 1) % count, i) for i in range(ends)])  29.9 us
    dot_general x3, matrix products, local(): jnp.dot(inverse_local, gathered, precision=HIGHEST, preferred_element_typ...  27.4 us
    ppermute x12, starting transfers between devices, extended_2(): lax.ppermute(head, axis, [((i + 1) % count, i) for i in range(ends)])  19.5 us
    gather x3, local copies, waits for them, and re-layouts, local(): gathered = residual_window.reshape(LOCAL, columns)[local_order]  10.9 us
  transfers between devices with their start and end apart: 24, of which 12 were waited for; matrix products, arithmetic and copies ran while one was open for 2% of the time, Pallas kernels for 0%

commit v1 on v0

v1 whole, which is shorter than its diff:
```python
import functools
import math

import jax
import jax.numpy as jnp
from jax import lax
from jax.experimental import pallas as pl
from jax.experimental.pallas import tpu as pltpu
from jax.sharding import PartitionSpec as P

ITERS = 3
REACTION = 0.01
LANES = 128
SUB = 8
F32 = jnp.float32
BF16 = jnp.bfloat16
MESH = pl.DeviceIdType.MESH
DIRS = ((-1, -1), (-1, 0), (-1, 1), (0, -1), (0, 1), (1, -1), (1, 0), (1, 1))


def split(value):
    high = value.astype(BF16)
    return high, (value - high.astype(F32)).astype(BF16)


def dot(left, right):
    return jnp.dot(left, right, preferred_element_type=F32)


def dot3(left_high, left_low, right_high, right_low):
    return dot(left_high, right_high) + (dot(left_low, right_high) + dot(left_high, right_low))


def kernel(
    cfg,
    rhs_ref,
    guess_ref,
    cond_ref,
    wrow_ref,
    wcol_ref,
    inv_hbm,
    basis_ref,
    bexp_ref,
    coarse_ref,
    sol_out,
    res_out,
    inv_v,
    perm,
    perm_t,
    t_high,
    t_low,
    l_high,
    l_low,
    x0,
    d0,
    weights,
    phi_high,
    phi_low,
    bw,
    x_high,
    x_low,
    res,
    sol,
    img,
    deep,
    wdeep,
    z,
    kmat,
    g0,
    g,
    row0,
    col0,
    cs0,
    cor0,
    row1,
    col1,
    cs1,
    cor1,
    ssem,
    rsem,
    gs,
    gr,
    fs,
    fr,
    lsem,
):
    N, W, ES, OV, CS, COLS, MODES, KR = cfg
    H = OV + 1
    lo, hi = OV, OV + CS - H
    LOCAL = ES * ES
    DW = ES + 2 * SUB
    DH = ES + 2
    HALF = N // 2
    CHIPS = HALF * W
    a = lax.axis_index("narrow")
    b = lax.axis_index("wide")
    core = lax.rem(a, 2)
    me = (a // 2) * W + b

    def other(k):
        idx = lax.rem(me + k, CHIPS)
        return idx, (lax.rem(idx, W), 2 * (idx // W) + core)

    def valid(d):
        da, db = DIRS[d]
        return (a + da >= 0) & (a + da < N) & (b + db >= 0) & (b + db < W)

    barrier = pltpu.get_barrier_semaphore()

    def greet(k, carry):
        pl.semaphore_signal(barrier, inc=1, device_id=other(k)[1], device_id_type=MESH)
        return carry

    lax.fori_loop(1, CHIPS, greet, 0)
    count = CHIPS - 1
    for d, (da, db) in enumerate(DIRS):
        if da != 0:
            ok = valid(d)
            count = count + ok.astype(jnp.int32)

            @pl.when(ok)
            def _():
                pl.semaphore_signal(barrier, inc=1, device_id=(b + db, a + da), device_id_type=MESH)

    load = pltpu.make_async_copy(inv_hbm, inv_v, lsem)
    load.start()

    for d, (da, db) in enumerate(DIRS):

        @pl.when(jnp.logical_not(valid(d)))
        def _():
            for slot in range(ITERS + 1):
                if slot == 0:
                    rr, cc, kk = row0, col0, cor0
                else:
                    rr, cc, kk = row1.at[slot - 1], col1.at[slot - 1], cor1.at[slot - 1]
                if db == 0:
                    ref = rr.at[(da + 1) // 2]
                elif da == 0:
                    ref = cc.at[(db + 1) // 2]
                else:
                    ref = kk.at[(da + 1) + (db + 1) // 2]
                ref[...] = jnp.zeros(ref.shape, F32)

    step = 256

    def hot(i, carry):
        off = pl.multiple_of(i * step, step)
        pos = lax.broadcasted_iota(jnp.int32, (step, LOCAL), 0) + off
        perm[pl.ds(off, step), :] = jnp.where(pos == wrow_ref[...], 1.0, 0.0).astype(BF16)
        lane = lax.broadcasted_iota(jnp.int32, (step, LOCAL), 1)
        perm_t[pl.ds(off, step), :] = jnp.where(
            lane == wcol_ref[pl.ds(off, step), :], 1.0, 0.0
        ).astype(BF16)
        return carry

    lax.fori_loop(0, LOCAL // step, hot, 0)
    b_high, b_low = split(bexp_ref[...])
    packed = dot(perm[...], b_high) + dot(perm[...], b_low)
    x0[:, :, 2 * COLS :] = packed.reshape(ES, ES, LANES)
    last = lax.broadcasted_iota(jnp.int32, (CS, LANES), 1) == LANES - 1

    def fill(i, carry):
        u = OV + i
        x0[u, OV : OV + CS, 0:COLS] = guess_ref[i]
        x0[u, OV : OV + CS, COLS : 2 * COLS] = rhs_ref[i]
        x0[u, OV : OV + CS, 2 * COLS :] = jnp.where(
            last, cond_ref[i], x0[u, OV : OV + CS, 2 * COLS :]
        )
        return carry

    lax.fori_loop(0, CS, fill, 0)

    def strips(slot, src, rr, cc, cs, kk):
        copies = []
        for d, (da, db) in enumerate(DIRS):
            rows = pl.ds(hi if da > 0 else lo, H)
            if db == 0:
                part, dst = src.at[rows], rr.at[(1 - da) // 2]
            elif da == 0:
                part, dst = cs.at[(db + 1) // 2], cc.at[(1 - db) // 2]
            else:
                part = src.at[rows, pl.ds(ES - SUB if db > 0 else 0, SUB)]
                dst = kk.at[(1 - da) + (1 - db) // 2]
            copies.append(
                pltpu.make_async_remote_copy(
                    src_ref=part,
                    dst_ref=dst,
                    send_sem=ssem.at[slot, d],
                    recv_sem=rsem.at[slot, 7 - d],
                    device_id=(b + db, a + da),
                    device_id_type=MESH,
                )
            )
        return copies

    def pack(src, cs):
        def body(u, carry):
            for j in range(H):
                cs[0, j, pl.ds(u, 1), :] = src[u, lo + j : lo + j + 1, :]
                cs[1, j, pl.ds(u, 1), :] = src[u, hi + j : hi + j + 1, :]
            return carry

        lax.fori_loop(0, ES, body, 0)

    def send_strips(copies):
        for d in (3, 4, 1, 6, 0, 2, 5, 7):

            @pl.when(valid(d))
            def _():
                copies[d].start()

    def recv_strips(copies):
        for d in range(8):

            @pl.when(valid(d))
            def _():
                copies[7 - d].wait_recv()

    def done_strips(copies):
        for d in range(8):

            @pl.when(valid(d))
            def _():
                copies[d].wait_send()

    def unpack(dst, src, rr, cc, kk):
        def centre(i, carry):
            u = OV + i
            dst[u + 1, SUB : SUB + ES, :] = src[u]
            for j in range(H):
                p = SUB - 1 + j
                dst[u + 1, p : p + 1, :] = cc[0, j, pl.ds(u, 1), :]
                p = SUB + CS + OV + j
                dst[u + 1, p : p + 1, :] = cc[1, j, pl.ds(u, 1), :]
            return carry

        lax.fori_loop(0, CS, centre, 0)
        own = slice(OV, OV + CS)
        left, right = SUB - 1, SUB + CS + OV
        base = hi - (ES - SUB)
        for side, top in ((0, 0), (1, CS + H)):
            for j in range(H):
                dst[top + j, SUB + OV : SUB + OV + CS, :] = rr[side, j, own, :]
                dst[top + j, left : left + H, :] = kk[2 * side, j, base : base + H, :]
                dst[top + j, right : right + H, :] = kk[2 * side + 1, j, lo : lo + H, :]

    def coarse_copy(slot, k, ref):
        _, target = other(k)
        return pltpu.make_async_remote_copy(
            src_ref=ref.at[a, b],
            dst_ref=ref.at[a, b],
            send_sem=gs.at[slot, k],
            recv_sem=gr.at[slot, me],
            device_id=target,
            device_id_type=MESH,
        )

    def coarse_send(slot, ref):
        def body(k, carry):
            coarse_copy(slot, k, ref).start()
            return carry

        lax.fori_loop(1, CHIPS, body, 0)

    def forward(slot, i, ref):
        return pltpu.make_async_remote_copy(
            src_ref=ref.at[2 * i + core],
            dst_ref=ref.at[2 * i + core],
            send_sem=fs.at[slot, i],
            recv_sem=fr.at[slot, i],
            device_id=(b, a + 1 - 2 * core),
            device_id_type=MESH,
        )

    def coarse_relay(slot, ref):
        def body(k, carry):
            idx, target = other(k)
            pltpu.make_async_remote_copy(
                src_ref=ref.at[a, b],
                dst_ref=ref.at[target[1], target[0]],
                send_sem=gs.at[slot, k],
                recv_sem=gr.at[slot, idx],
                device_id=target,
                device_id_type=MESH,
            ).wait_recv()
            return carry

        lax.fori_loop(1, CHIPS, body, 0)
        for i in range(HALF):
            forward(slot, i, ref).start()

    def coarse_recv(slot, ref):
        for i in range(HALF):
            pltpu.make_async_remote_copy(
                src_ref=ref.at[2 * i + core],
                dst_ref=ref.at[2 * i + 1 - core],
                send_sem=fs.at[slot, i],
                recv_sem=fr.at[slot, i],
                device_id=(b, a + 1 - 2 * core),
                device_id_type=MESH,
            ).wait_recv()

    def coarse_done(slot, ref):
        def body(k, carry):
            coarse_copy(slot, k, ref).wait_send()
            return carry

        lax.fori_loop(1, CHIPS, body, 0)
        for i in range(HALF):
            forward(slot, i, ref).wait_send()

    first = strips(0, x0, row0, col0, cs0, cor0)
    pack(x0, cs0)
    pl.semaphore_wait(barrier, count)
    send_strips(first)

    load.wait()

    def right_side_perm(i, carry):
        rows = pl.ds(pl.multiple_of(i * step, step), step)
        high, low = split(inv_v[rows, :])
        t_high[rows, :] = dot(high, perm_t[...]).astype(BF16)
        t_low[rows, :] = dot(low, perm_t[...]).astype(BF16)
        return carry

    lax.fori_loop(0, LOCAL // step, right_side_perm, 0)

    def left_side_perm(i, carry):
        rows = pl.ds(pl.multiple_of(i * step, step), step)
        l_high[rows, :] = dot(perm[rows, :], t_high[...]).astype(BF16)
        l_low[rows, :] = dot(perm[rows, :], t_low[...]).astype(BF16)
        return carry

    lax.fori_loop(0, LOCAL // step, left_side_perm, 0)
    m_high, m_low = split(basis_ref[...])
    bw[0] = dot(m_high, perm_t[...]).astype(BF16)
    bw[1] = dot(m_low, perm_t[...]).astype(BF16)

    d0[...] = jnp.zeros(d0.shape, F32)
    recv_strips(first)
    unpack(d0, x0, row0, col0, cor0)

    def modes(u, carry):
        value = d0[u, :, 2 * COLS :]
        high, low = split(value)
        rows = pl.ds(pl.multiple_of(u * DW, DW), DW)
        phi_high[rows, :] = high
        phi_low[rows, :] = low
        d0[u, :, 2 * COLS :] = jnp.broadcast_to(value[:, LANES - 1 : LANES], (DW, LANES))
        return carry

    lax.fori_loop(0, DH, modes, 0)
    col_pos = b * CS - OV + lax.broadcasted_iota(jnp.int32, (ES, LANES), 0)
    col_in = jnp.where((col_pos >= 0) & (col_pos < CS * W), 1.0, 0.0)

    def faces(u, carry):
        row_pos = a * CS - OV + u
        inside = jnp.where((row_pos >= 0) & (row_pos < CS * N), col_in, 0.0)
        cond = lambda du, dt: d0[u + 1 + du, SUB + dt : SUB + dt + ES, 2 * COLS :]
        own = cond(0, 0)
        half = 0.5 * inside
        weights[0, u] = REACTION * inside
        weights[1, u] = half * (own + cond(-1, 0))
        weights[2, u] = half * (own + cond(1, 0))
        weights[3, u] = half * (own + cond(0, -1))
        weights[4, u] = half * (own + cond(0, 1))
        return carry

    lax.fori_loop(0, ES, faces, 0)

    def operator(ref, u):
        parts = []
        for c in range(0, COLS, LANES):
            at = lambda du, dt: ref[u + 1 + du, SUB + dt : SUB + dt + ES, c : c + LANES]
            mid = at(0, 0)
            parts.append(
                weights[0, u] * mid
                + weights[1, u] * (mid - at(-1, 0))
                + weights[2, u] * (mid - at(1, 0))
                + weights[3, u] * (mid - at(0, -1))
                + weights[4, u] * (mid - at(0, 1))
            )
        return jnp.concatenate(parts, axis=1)

    def set_x(u, value):
        high, low = split(value)
        rows = pl.ds(pl.multiple_of(u * ES, ES), ES)
        x_high[rows, :] = high
        x_low[rows, :] = low

    def first_residual(u, carry):
        inside = jnp.where(weights[0, u] > 0.0, 1.0, 0.0)
        inside = jnp.concatenate([inside] * (COLS // LANES), axis=1)
        right = d0[u + 1, SUB : SUB + ES, COLS : 2 * COLS]
        value = right * inside - operator(d0, u)
        res[u] = value
        set_x(u, value)
        return carry

    lax.fori_loop(0, ES, first_residual, 0)

    def start_sol(i, carry):
        sol[i] = d0[OV + i + 1, SUB : SUB + ES, 0:COLS]
        return carry

    lax.fori_loop(0, CS, start_sol, 0)

    def coarse_rows():
        return dot3(bw[0], bw[1], x_high[...], x_low[...])

    sub_pos = lax.broadcasted_iota(jnp.int32, (SUB, COLS), 0)
    wdeep[...] = jnp.zeros(wdeep.shape, F32)
    pending = []
    numer = denom = None
    for it in range(ITERS + 1):
        ref = g0 if it == 0 else g.at[it - 1]
        if it == 0:
            ref[a, b] = jnp.zeros((ref.shape[2], COLS), F32)
            ref[a, b, 0:SUB, :] = coarse_rows()
            ref[a, b, MODES : MODES + KR, :] = coarse_ref[...]
        else:
            rows = coarse_rows() if it < ITERS else jnp.zeros((SUB, COLS), F32)
            rows = jnp.where(sub_pos == MODES, numer, rows)
            rows = jnp.where(sub_pos == MODES + 1, denom, rows)
            ref[a, b] = rows
        coarse_send(it, ref)
        if it < ITERS:

            def solve(i, carry):
                rows = pl.ds(pl.multiple_of(i * step, step), step)
                value = dot3(l_high[rows, :], l_low[rows, :], x_high[...], x_low[...])
                z[it, pl.ds(i * (step // ES), step // ES)] = value.reshape(step // ES, ES, COLS)
                return carry

            lax.fori_loop(0, LOCAL // step, solve, 0)
            pack(z.at[it], cs1.at[it])
            copies = strips(it + 1, z.at[it], row1.at[it], col1.at[it], cs1.at[it], cor1.at[it])
            send_strips(copies)
            pending.append(copies)
        coarse_relay(it, ref)
        coarse_recv(it, ref)
        if it == 0:
            per = COLS // (4 * W)
            wide_cols = MODES * W
            group = MODES * N
            piece = lax.broadcasted_iota(jnp.int32, (group, COLS), 0) & (per - 1)
            lane = lax.broadcasted_iota(jnp.int32, (group, COLS), 1)
            keep = (lane >> int(math.log2(wide_cols))) == piece
            width = N * W * SUB
            j = lax.broadcasted_iota(jnp.int32, (COLS, width), 0) & (wide_cols - 1)
            c = lax.broadcasted_iota(jnp.int32, (COLS, width), 1)
            total_high = total_low = None
            for a2 in range(N):
                blocks = []
                for third in range(3):
                    db = lax.rem(third - b + 1 + 3 * W, 3) - 1
                    at = jnp.clip(b + db, 0, W - 1)
                    raw = ref[a2, at, MODES : MODES + KR, :]
                    tall = jnp.concatenate(
                        [jnp.broadcast_to(raw[r : r + 1], (per, COLS)) for r in range(KR)], axis=0
                    )
                    blocks.append(jnp.where(keep, tall, 0.0))
                blocks.append(jnp.zeros((LANES - 3 * group, COLS), F32))
                high, low = split(jnp.concatenate(blocks, axis=0))
                fold = c == a2 * (W * SUB) + (j >> 2) * SUB + (j & 3)
                fold = jnp.where(fold, 1.0, 0.0).astype(BF16)
                th, tl = dot(high, fold), dot(low, fold)
                total_high = th if total_high is None else total_high + th
                total_low = tl if total_low is None else total_low + tl
            kmat[0] = total_high.astype(BF16)
            kmat[1] = total_low.astype(BF16)
        else:
            total = jnp.sum(ref[...].reshape(N * W, SUB, COLS), axis=0)
            size = total[MODES : MODES + 1] / total[MODES + 1 : MODES + 2]
        if it == ITERS:
            break
        g_high, g_low = split(ref[:, :, 0:SUB, :].reshape(N * W * SUB, COLS))
        s_high, s_low = split(dot3(kmat[0], kmat[1], g_high, g_low))
        recv_strips(copies)
        unpack(wdeep, z.at[it], row1.at[it], col1.at[it], cor1.at[it])

        if it > 0:

            def advance(i, carry):
                u = OV + i
                sol[i] = sol[i] + size * deep[u + 1, SUB : SUB + ES, :]
                res[u] = res[u] - size * img[u]
                return carry

            lax.fori_loop(0, CS, advance, 0)
        chunk = DH // 2

        def coarse_part(i, carry):
            rows = pl.ds(pl.multiple_of(i * chunk * DW, chunk * DW), chunk * DW)
            value = dot3(phi_high[rows, :], phi_low[rows, :], s_high, s_low)
            tall = pl.ds(i * chunk, chunk)
            value = value.reshape(chunk, DW, COLS) + wdeep[tall]
            if it == 0:
                deep[tall] = value
            else:
                deep[tall] = deep[tall] - size * value
            return carry

        lax.fori_loop(0, 2, coarse_part, 0)

        def apply(u, carry):
            top, bottom = carry
            value = operator(deep, u)
            img[u] = value
            if it < ITERS - 1:
                set_x(u, value)
            own = jnp.where((u >= OV) & (u < OV + CS), value, 0.0)
            return top + res[u] * own, bottom + value * own

        nothing = jnp.zeros((ES, COLS), F32)
        top, bottom = lax.fori_loop(0, ES, apply, (nothing, nothing))
        col = lax.broadcasted_iota(jnp.int32, (ES, COLS), 0)
        mine = (col >= OV) & (col < OV + CS)
        numer = jnp.sum(jnp.where(mine, top, 0.0), axis=0, keepdims=True)
        denom = jnp.sum(jnp.where(mine, bottom, 0.0), axis=0, keepdims=True)

    def finish(i, carry):
        u = OV + i
        sol_out[i] = (sol[i] + size * deep[u + 1, SUB : SUB + ES, :])[OV : OV + CS]
        res_out[i] = (res[u] - size * img[u])[OV : OV + CS]
        return carry

    lax.fori_loop(0, CS, finish, 0)
    done_strips(first)
    for copies in pending:
        done_strips(copies)
    for it in range(ITERS + 1):
        coarse_done(it, g0 if it == 0 else g.at[it - 1])


def local(
    N,
    W,
    right_side,
    initial_guess,
    class_map,
    class_conductivity,
    window_index,
    local_inverse,
    coarse_basis,
    coarse_inverse,
):
    CS, _, COLS = right_side.shape
    MODES, LOCAL = coarse_basis.shape[2:]
    ES = math.isqrt(LOCAL)
    OV = (ES - CS) // 2
    H = OV + 1
    DW, DH = ES + 2 * SUB, ES + 2
    KR = coarse_inverse.size // COLS
    R0 = -(-(MODES + KR) // SUB) * SUB
    CHIPS = N * W // 2
    classes = class_conductivity.shape[0]
    matches = class_map[:, :, None] == jnp.arange(classes, dtype=jnp.int32)[None, None, :]
    conduct = jnp.sum(jnp.where(matches, class_conductivity[None, None, :], 0.0), axis=2)
    conduct = jnp.broadcast_to(conduct[:, :, None], (CS, CS, LANES))
    basis = coarse_basis[0, 0]
    place = lax.rem(lax.axis_index("wide"), 3) * (MODES * N) + lax.axis_index("narrow") * MODES
    lane = jnp.arange(LANES, dtype=jnp.int32)[None, :] - place
    turned = basis.T
    spread = sum(jnp.where(lane == m, turned[:, m : m + 1], 0.0) for m in range(MODES))
    padded = jnp.concatenate([basis, jnp.zeros((SUB - MODES, LOCAL), F32)], axis=0)
    vmem = pl.BlockSpec(memory_space=pltpu.VMEM)
    big = 2 * COLS + LANES
    scratch = [
        pltpu.VMEM((LOCAL, LOCAL), F32),
        pltpu.VMEM((LOCAL, LOCAL), BF16),
        pltpu.VMEM((LOCAL, LOCAL), BF16),
        pltpu.VMEM((LOCAL, LOCAL), BF16),
        pltpu.VMEM((LOCAL, LOCAL), BF16),
        pltpu.VMEM((LOCAL, LOCAL), BF16),
        pltpu.VMEM((LOCAL, LOCAL), BF16),
        pltpu.VMEM((ES, ES, big), F32),
        pltpu.VMEM((DH, DW, big), F32),
        pltpu.VMEM((5, ES, ES, LANES), F32),
        pltpu.VMEM((DH * DW, LANES), BF16),
        pltpu.VMEM((DH * DW, LANES), BF16),
        pltpu.VMEM((2, SUB, LOCAL), BF16),
        pltpu.VMEM((LOCAL, COLS), BF16),
        pltpu.VMEM((LOCAL, COLS), BF16),
        pltpu.VMEM((ES, ES, COLS), F32),
        pltpu.VMEM((CS, ES, COLS), F32),
        pltpu.VMEM((ES, ES, COLS), F32),
        pltpu.VMEM((DH, DW, COLS), F32),
        pltpu.VMEM((DH, DW, COLS), F32),
        pltpu.VMEM((ITERS, ES, ES, COLS), F32),
        pltpu.VMEM((2, LANES, N * W * SUB), BF16),
        pltpu.VMEM((N, W, R0, COLS), F32),
        pltpu.VMEM((ITERS, N, W, SUB, COLS), F32),
        pltpu.VMEM((2, H, ES, big), F32),
        pltpu.VMEM((2, H, ES, big), F32),
        pltpu.VMEM((2, H, ES, big), F32),
        pltpu.VMEM((4, H, SUB, big), F32),
        pltpu.VMEM((ITERS, 2, H, ES, COLS), F32),
        pltpu.VMEM((ITERS, 2, H, ES, COLS), F32),
        pltpu.VMEM((ITERS, 2, H, ES, COLS), F32),
        pltpu.VMEM((ITERS, 4, H, SUB, COLS), F32),
        pltpu.SemaphoreType.DMA((ITERS + 1, 8)),
        pltpu.SemaphoreType.DMA((ITERS + 1, 8)),
        pltpu.SemaphoreType.DMA((ITERS + 1, CHIPS)),
        pltpu.SemaphoreType.DMA((ITERS + 1, CHIPS)),
        pltpu.SemaphoreType.DMA((ITERS + 1, N // 2)),
        pltpu.SemaphoreType.DMA((ITERS + 1, N // 2)),
        pltpu.SemaphoreType.DMA,
    ]
    out = jax.ShapeDtypeStruct(right_side.shape, F32)
    return pl.pallas_call(
        functools.partial(kernel, (N, W, ES, OV, CS, COLS, MODES, KR)),
        out_shape=(out, out),
        in_specs=[vmem] * 5 + [pl.BlockSpec(memory_space=pl.ANY)] + [vmem] * 3,
        out_specs=(vmem, vmem),
        scratch_shapes=scratch,
        compiler_params=pltpu.CompilerParams(
            collective_id=0, has_side_effects=True, vmem_limit_bytes=67043328
        ),
        name="schwarz",
    )(
        right_side,
        initial_guess,
        conduct,
        window_index.reshape(1, LOCAL),
        window_index.reshape(LOCAL, 1),
        local_inverse[0, 0],
        padded,
        spread,
        coarse_inverse.reshape(KR, COLS),
    )


def solution(mesh):
    in_specs = (
        P("narrow", "wide", None),
        P("narrow", "wide", None),
        P("narrow", "wide"),
        P(),
        P("narrow", "wide", None),
        P("narrow", "wide", None, None),
        P("narrow", "wide", None, None),
        P("wide", "narrow"),
    )
    out_specs = (P("narrow", "wide", None), P("narrow", "wide", None))
    body = functools.partial(local, mesh.shape["narrow"], mesh.shape["wide"])
    return jax.shard_map(body, mesh=mesh, in_specs=in_specs, out_specs=out_specs, check_vma=False)
```

time: 429 us -> 91.5 us (0.21)
  blocking collectives: 246 us -> 0 us
  Pallas kernels: 0 us -> 77.3 us
  starting transfers between devices: 60.4 us -> 0 us
  matrix products: 33 us -> 0 us
  waiting for transfers between devices: 32.1 us -> 0 us
  other arithmetic: 25.5 us -> 2.26 us
  local copies, waits for them, and re-layouts: 27.3 us -> 10.7 us
    psum x3 -> x0, blocking collectives: 114 us -> none  [local(): lax.psum((jnp.sum(residual_window[OV:OV + CS, OV:OV + CS] * image, axis=(...]
    pallas_call x0 -> x1, Pallas kernels: none -> 77.3 us  [local(): pl.pallas_call(functools.partial(kernel, (N, W, ES, OV, CS, COLS, MODES,...]
    all_gather x3 -> x0, blocking collectives: 75.4 us -> none  [local(): lax.all_gather(coarse_rhs[None], 'wide', axis=0, tiled=True)]
    ppermute x24 -> x0, starting transfers between devices: 60.4 us -> none  [the longest x12 40.9 us: extended_2(): lax.ppermute(tail, axis, [(i, (i + 1) % count) for i in range(ends)])]
    unnamed x3 -> x0, blocking collectives: 56 us -> none
    dot_general x12 -> x0, matrix products: 33 us -> none  [the longest x3 27.4 us: local(): jnp.dot(inverse_local, gathered, precision=HIGHEST, preferred_element_typ...]
    ppermute x24 -> x0, waiting for transfers between devices: 32.1 us -> none  [the longest x12 29.9 us: extended_2(): lax.ppermute(head, axis, [((i + 1) % count, i) for i in range(ends)])]
    gather x6 -> x0, local copies, waits for them, and re-layouts: 21.3 us -> none  [the longest x3 10.9 us: local(): gathered = residual_window.reshape(LOCAL, columns)[local_order]]
  transfers between devices with their start and end apart: 24 -> 0, of which waited for: 12 -> 0; matrix products, arithmetic and copies ran while one was open for 2% -> 0% of each run, Pallas kernels for 0% -> 0%
where the time goes in v1:
time: 91.5 us; the launch traced here: 90.9 us
  Pallas kernels  77.3 us (84%)
  local copies, waits for them, and re-layouts  10.7 us (12%)
  other arithmetic  2.26 us (2%)
    pallas_call x1, Pallas kernels, local(): pl.pallas_call(functools.partial(kernel, (N, W, ES, OV, CS, COLS, MODES,...  77.3 us
    unnamed x2, local copies, waits for them, and re-layouts  4.4 us

profile of v1, /device:TPU:1, one launch (start us, length us, event | category | flops | bytes accessed | tf_op | source)
XLA Modules:
  0.0 90.9 jit_solution(14067416850638787312)
XLA Ops:
  0.7 1.4 %reshape.34.coarse_ref = f32[2,256]{1,0:T(2,128)} reshape(f32[16,32]{1,0:T(8,128)} %param.15) | data formatting | bytes 4096 | tf_op jit(solution)/shard_map/reshape | solution.py:631
  2.0 0.8 select_reduce_fusion
  2.9 0.9 fusion.4
  3.8 1.3 %concatenate.3.basis_ref = f32[8,1024]{1,0:T(8,128)} pad(f32[4,1024]{1,0:T(4,128)} %bitcast.12, f32[]{:T(128)} %constant.10.clone.1), padding=0_4x0_0 | pad | bytes 49156 | tf_op jit(solution)/shard_map/concatenate | solution.py:567
  5.1 1.0 %broadcast_in_dim.86.cond_ref = f32[28,28,128]{2,1,0:T(8,128)} broadcast(f32[28,28]{1,0:T(8,128)S(1)} %select_reduce_fusion), dimensions={0,1} | broadcast | bytes 404544 | tf_op jit(solution)/shard_map/broadcast_in_dim | solution.py:561
  6.1 1.4 %select_add_fusion.bexp_ref = f32[1024,128]{1,0:T(8,128)} fusion(f32[1024]{0:T(1024)S(1)} %bitcast.16, f32[1024]{0:T(1024)S(1)} %bitcast.17, f32[1024]{0:T(1024)S(1)} %bitcast.18, f32[1024]{0:T(1024)S(1)} %bitcast.15, pred[128]{0:T(512)(128)(4,1)S(1)} %get-tuple-element.6, pred[128]{0:T(512)(128)(4,1)S(1)} %get-tuple-element.7, ...), kind=kLoop, calls=%fused_computation | loop fusion | flops 917504 | bytes 541184 | tf_op jit(solution)/shard_map/add | solution.py:566
  7.5 1.7 %copy.11.wcol_ref = s32[1024,1]{1,0:T(8,128)} copy(s32[1024,1]{0,1:T(1,128)} %bitcast.13) | data formatting | bytes 8192 | tf_op jit(solution)/shard_map/reshape | solution.py:627
  9.2 77.3 %schwarz.1 = (f32[28,28,256]{2,1,0:T(8,128)}, f32[28,28,256]{2,1,0:T(8,128)}) custom-call(f32[28,28,256]{2,1,0:T(8,128)} %rhs_ref.1, f32[28,28,256]{2,1,0:T(8,128)} %guess_ref.1, f32[28,28,128]{2,1,0:T(8,128)} %broadcast_in_dim.86.cond_ref, s32[1,1024]{1,0:T(1,128)} %bitcast.14, s32[1024,1]{1,0:T(8,128)} %copy.11.wcol_ref, f32[1024,1024]{1,0:T(8,128)} %bitcast.10, ...), custom_call_target="tpu_custom_call" | custom-call | tf_op jit(solution)/shard_map/schwarz/pallas_call | solution.py:612
  86.5 2.2 %copy.14 = f32[28,28,256]{2,1,0:T(8,128)} copy(f32[28,28,256]{2,1,0:T(8,128)} %get-tuple-element.12) | data formatting | bytes 1605632
  88.7 2.2 %copy.15 = f32[28,28,256]{2,1,0:T(8,128)} copy(f32[28,28,256]{2,1,0:T(8,128)} %get-tuple-element.13) | data formatting | bytes 1605632
  (2 shorter events, 0.0 us)

commit v2 on v1

--- a/solution.py
+++ b/solution.py
@@ -35,15 +35,17 @@
     cfg,
     rhs_ref,
     guess_ref,
-    cond_ref,
+    map_ref,
+    class_ref,
     wrow_ref,
-    wcol_ref,
     inv_hbm,
     basis_ref,
-    bexp_ref,
     coarse_ref,
     sol_out,
+    dir_out,
     res_out,
+    img_out,
+    size_out,
     inv_v,
     perm,
     perm_t,
@@ -83,6 +85,9 @@
     fs,
     fr,
     lsem,
+    osem,
+    field,
+    spread,
 ):
     N, W, ES, OV, CS, COLS, MODES, KR = cfg
     H = OV + 1
@@ -143,29 +148,45 @@
                 ref[...] = jnp.zeros(ref.shape, F32)
 
     step = 256
+    numbering = wrow_ref[...]
+    tall_numbering = jnp.transpose(jnp.broadcast_to(numbering, (LANES, LOCAL)))
+    lane = lax.broadcasted_iota(jnp.int32, (LOCAL, LANES), 1)
+    for c in range(0, LOCAL, LANES):
+        perm_t[:, c : c + LANES] = jnp.where(lane + c == tall_numbering, 1.0, 0.0).astype(BF16)
 
     def hot(i, carry):
         off = pl.multiple_of(i * step, step)
         pos = lax.broadcasted_iota(jnp.int32, (step, LOCAL), 0) + off
-        perm[pl.ds(off, step), :] = jnp.where(pos == wrow_ref[...], 1.0, 0.0).astype(BF16)
-        lane = lax.broadcasted_iota(jnp.int32, (step, LOCAL), 1)
-        perm_t[pl.ds(off, step), :] = jnp.where(
-            lane == wcol_ref[pl.ds(off, step), :], 1.0, 0.0
-        ).astype(BF16)
+        perm[pl.ds(off, step), :] = jnp.where(pos == numbering, 1.0, 0.0).astype(BF16)
         return carry
 
     lax.fori_loop(0, LOCAL // step, hot, 0)
-    b_high, b_low = split(bexp_ref[...])
+    basis = basis_ref[0, 0]
+    place = lax.rem(b, 3) * (MODES * N) + a * MODES
+    line = lax.broadcasted_iota(jnp.int32, (LANES, LOCAL), 0) - place
+    spread[...] = jnp.zeros(spread.shape, F32)
+    for m in range(MODES):
+        spread[...] = jnp.where(line == m, basis[m : m + 1], spread[...])
+    b_high, b_low = split(jnp.transpose(spread[...]))
     packed = dot(perm[...], b_high) + dot(perm[...], b_low)
     x0[:, :, 2 * COLS :] = packed.reshape(ES, ES, LANES)
+    classes = map_ref[...]
+    conduct = jnp.zeros(classes.shape, F32)
+    for k in range(class_ref.shape[0]):
+        conduct = jnp.where(classes == k, class_ref[k], conduct)
+    field[...] = jnp.zeros(field.shape, F32)
+    field[0:CS, 0:CS] = conduct
+    turned = jnp.transpose(field[...])[0:ES]
+    lanes = lax.broadcasted_iota(jnp.int32, (ES, LANES), 1)
     last = lax.broadcasted_iota(jnp.int32, (CS, LANES), 1) == LANES - 1
 
     def fill(i, carry):
         u = OV + i
+        column = jnp.sum(jnp.where(lanes == i, turned, 0.0), axis=1, keepdims=True)
         x0[u, OV : OV + CS, 0:COLS] = guess_ref[i]
         x0[u, OV : OV + CS, COLS : 2 * COLS] = rhs_ref[i]
         x0[u, OV : OV + CS, 2 * COLS :] = jnp.where(
-            last, cond_ref[i], x0[u, OV : OV + CS, 2 * COLS :]
+            last, column[0:CS], x0[u, OV : OV + CS, 2 * COLS :]
         )
         return carry
 
@@ -314,6 +335,8 @@
     pack(x0, cs0)
     pl.semaphore_wait(barrier, count)
     send_strips(first)
+    d0[...] = jnp.zeros(d0.shape, F32)
+    wdeep[...] = jnp.zeros(wdeep.shape, F32)
 
     load.wait()
 
@@ -333,11 +356,10 @@
         return carry
 
     lax.fori_loop(0, LOCAL // step, left_side_perm, 0)
-    m_high, m_low = split(basis_ref[...])
+    m_high, m_low = split(jnp.concatenate([basis, jnp.zeros((SUB - MODES, LOCAL), F32)], axis=0))
     bw[0] = dot(m_high, perm_t[...]).astype(BF16)
     bw[1] = dot(m_low, perm_t[...]).astype(BF16)
 
-    d0[...] = jnp.zeros(d0.shape, F32)
     recv_strips(first)
     unpack(d0, x0, row0, col0, cor0)
 
@@ -410,7 +432,6 @@
         return dot3(bw[0], bw[1], x_high[...], x_low[...])
 
     sub_pos = lax.broadcasted_iota(jnp.int32, (SUB, COLS), 0)
-    wdeep[...] = jnp.zeros(wdeep.shape, F32)
     pending = []
     numer = denom = None
     for it in range(ITERS + 1):
@@ -418,13 +439,29 @@
         if it == 0:
             ref[a, b] = jnp.zeros((ref.shape[2], COLS), F32)
             ref[a, b, 0:SUB, :] = coarse_rows()
-            ref[a, b, MODES : MODES + KR, :] = coarse_ref[...]
+            run = MODES * W
+            for i in range(MODES * N):
+                line, at = divmod(i * run, COLS)
+                ref[a, b, MODES + line, at : at + run] = coarse_ref[i]
         else:
             rows = coarse_rows() if it < ITERS else jnp.zeros((SUB, COLS), F32)
             rows = jnp.where(sub_pos == MODES, numer, rows)
             rows = jnp.where(sub_pos == MODES + 1, denom, rows)
             ref[a, b] = rows
         coarse_send(it, ref)
+        if it == ITERS:
+            own = pl.ds(OV, CS)
+            pairs = (
+                (sol, sol_out),
+                (deep.at[pl.ds(OV + 1, CS), pl.ds(SUB, ES)], dir_out),
+                (res.at[own], res_out),
+                (img.at[own], img_out),
+            )
+            writes = [
+                pltpu.make_async_copy(src, dst, osem.at[n]) for n, (src, dst) in enumerate(pairs)
+            ]
+            for copy in writes:
+                copy.start()
         if it < ITERS:
 
             def solve(i, carry):
@@ -520,18 +557,21 @@
         numer = jnp.sum(jnp.where(mine, top, 0.0), axis=0, keepdims=True)
         denom = jnp.sum(jnp.where(mine, bottom, 0.0), axis=0, keepdims=True)
 
-    def finish(i, carry):
-        u = OV + i
-        sol_out[i] = (sol[i] + size * deep[u + 1, SUB : SUB + ES, :])[OV : OV + CS]
-        res_out[i] = (res[u] - size * img[u])[OV : OV + CS]
-        return carry
-
-    lax.fori_loop(0, CS, finish, 0)
     done_strips(first)
     for copies in pending:
         done_strips(copies)
+    size_out[...] = jnp.broadcast_to(size, (SUB, COLS))
+    for copy in writes:
+        copy.wait()
     for it in range(ITERS + 1):
         coarse_done(it, g0 if it == 0 else g.at[it - 1])
+
+
+def finish(OV, CS, sol, direction, res, image, size, sol_out, res_out):
+    step = size[0:1]
+    for i in range(sol.shape[0]):
+        sol_out[i] = (sol[i] + step * direction[i])[OV : OV + CS]
+        res_out[i] = (res[i] - step * image[i])[OV : OV + CS]
 
 
 def local(
@@ -555,16 +595,6 @@
     KR = coarse_inverse.size // COLS
     R0 = -(-(MODES + KR) // SUB) * SUB
     CHIPS = N * W // 2
-    classes = class_conductivity.shape[0]
-    matches = class_map[:, :, None] == jnp.arange(classes, dtype=jnp.int32)[None, None, :]
-    conduct = jnp.sum(jnp.where(matches, class_conductivity[None, None, :], 0.0), axis=2)
-    conduct = jnp.broadcast_to(conduct[:, :, None], (CS, CS, LANES))
-    basis = coarse_basis[0, 0]
-    place = lax.rem(lax.axis_index("wide"), 3) * (MODES * N) + lax.axis_index("narrow") * MODES
-    lane = jnp.arange(LANES, dtype=jnp.int32)[None, :] - place
-    turned = basis.T
-    spread = sum(jnp.where(lane == m, turned[:, m : m + 1], 0.0) for m in range(MODES))
-    padded = jnp.concatenate([basis, jnp.zeros((SUB - MODES, LOCAL), F32)], axis=0)
     vmem = pl.BlockSpec(memory_space=pltpu.VMEM)
     big = 2 * COLS + LANES
     scratch = [
@@ -607,29 +637,44 @@
         pltpu.SemaphoreType.DMA((ITERS + 1, N // 2)),
         pltpu.SemaphoreType.DMA((ITERS + 1, N // 2)),
         pltpu.SemaphoreType.DMA,
+        pltpu.SemaphoreType.DMA((4,)),
+        pltpu.VMEM((LANES, LANES), F32),
+        pltpu.VMEM((LANES, LOCAL), F32),
     ]
-    out = jax.ShapeDtypeStruct(right_side.shape, F32)
-    return pl.pallas_call(
+    out = jax.ShapeDtypeStruct((CS, ES, COLS), F32)
+    anywhere = pl.BlockSpec(memory_space=pl.ANY)
+    smem = pl.BlockSpec(memory_space=pltpu.SMEM)
+    *fields, size = pl.pallas_call(
         functools.partial(kernel, (N, W, ES, OV, CS, COLS, MODES, KR)),
-        out_shape=(out, out),
-        in_specs=[vmem] * 5 + [pl.BlockSpec(memory_space=pl.ANY)] + [vmem] * 3,
-        out_specs=(vmem, vmem),
+        out_shape=(out,) * 4 + (jax.ShapeDtypeStruct((SUB, COLS), F32),),
+        in_specs=[vmem] * 3 + [smem, vmem, anywhere] + [vmem] * 2,
+        out_specs=(anywhere,) * 4 + (vmem,),
         scratch_shapes=scratch,
         compiler_params=pltpu.CompilerParams(
-            collective_id=0, has_side_effects=True, vmem_limit_bytes=67043328
+            collective_id=0, has_side_effects=True, vmem_limit_bytes=60 * 2**20
         ),
         name="schwarz",
     )(
         right_side,
         initial_guess,
-        conduct,
-        window_index.reshape(1, LOCAL),
-        window_index.reshape(LOCAL, 1),
+        class_map,
+        class_conductivity,
+        window_index[0],
         local_inverse[0, 0],
-        padded,
-        spread,
-        coarse_inverse.reshape(KR, COLS),
+        coarse_basis,
+        coarse_inverse,
     )
+    block = CS // 4
+    part = pl.BlockSpec((block, ES, COLS), lambda i: (i, 0, 0))
+    done = pl.BlockSpec((block, CS, COLS), lambda i: (i, 0, 0))
+    return pl.pallas_call(
+        functools.partial(finish, OV, CS),
+        grid=(CS // block,),
+        out_shape=(jax.ShapeDtypeStruct(right_side.shape, F32),) * 2,
+        in_specs=[part] * 4 + [pl.BlockSpec((SUB, COLS), lambda i: (0, 0))],
+        out_specs=(done, done),
+        name="finish",
+    )(*fields, size)
 
 
 def solution(mesh):

time: 91.5 us -> 83.1 us (0.908)
  local copies, waits for them, and re-layouts: 10.7 us -> 0 us
  Pallas kernels: 77.3 us -> 82.2 us
  other arithmetic: 2.26 us -> 0 us
    unnamed x2 -> x0, local copies, waits for them, and re-layouts: 4.4 us -> none
    pallas_call x0 -> x1, Pallas kernels: none -> 4.15 us  [local(): pl.pallas_call(functools.partial(finish, OV, CS), grid=(CS // block,), ou...]
    reshape x2 -> x0, local copies, waits for them, and re-layouts: 3.07 us -> none  [the longest x1 1.71 us: local(): window_index.reshape(LOCAL, 1)]
    add x1 -> x0, other arithmetic: 1.4 us -> none  [local(): sum((jnp.where(lane == m, turned[:, m:m + 1], 0.0) for m in range(MODES)))]
    concatenate x1 -> x0, local copies, waits for them, and re-layouts: 1.33 us -> none  [local(): jnp.concatenate([basis, jnp.zeros((SUB - MODES, LOCAL), F32)], axis=0)]
    broadcast_in_dim x1 -> x0, local copies, waits for them, and re-layouts: 0.97 us -> none  [local(): conduct = jnp.broadcast_to(conduct[:, :, None], (CS, CS, LANES))]
where the time goes in v2:
time: 83.1 us; the launch traced here: 82.8 us
  Pallas kernels  82.2 us (99%)
    pallas_call x1, Pallas kernels, local(): pl.pallas_call(functools.partial(kernel, (N, W, ES, OV, CS, COLS, MODES,...  78 us
    pallas_call x1, Pallas kernels, local(): pl.pallas_call(functools.partial(finish, OV, CS), grid=(CS // block,), ou...  4.15 us

profile of v2, /device:TPU:1, one launch (start us, length us, event | category | flops | bytes accessed | tf_op | source)
XLA Modules:
  0.0 82.8 jit_solution(1914187165129858597)
XLA Ops:
  0.6 78.0 %schwarz.1 = (f32[28,32,256]{2,1,0:T(8,128)}, f32[28,32,256]{2,1,0:T(8,128)}, f32[28,32,256]{2,1,0:T(8,128)}, f32[28,32,256]{2,1,0:T(8,128)}, f32[8,256]{1,0:T(8,128)}) custom-call(f32[28,28,256]{2,1,0:T(8,128)} %rhs_ref.1, f32[28,28,256]{2,1,0:T(8,128)} %guess_ref.1, s32[28,28]{1,0:T(8,128)} %map_ref.1, f32[8]{0:T(128)} %class_ref.1, s32[1,1024]{1,0:T(1,128)} %bitcast.3, ...), custom_call_target="tpu_custom_call" | custom-call | tf_op jit(solution)/shard_map/schwarz/pallas_call | solution.py:647
  78.7 4.2 %finish.1 = (f32[28,28,256]{2,1,0:T(8,128)}, f32[28,28,256]{2,1,0:T(8,128)}) custom-call(f32[28,32,256]{2,1,0:T(8,128)} %get-tuple-element.7.sol, f32[28,32,256]{2,1,0:T(8,128)} %get-tuple-element.8.direction, f32[28,32,256]{2,1,0:T(8,128)} %get-tuple-element.9.res, f32[28,32,256]{2,1,0:T(8,128)} %get-tuple-element.10.image, f32[8,256]{1,0:T(8,128)} %get-tuple-element.11.size), custom_call_target="tpu_custom_call" | custom-call | tf_op jit(solution)/shard_map/finish/pallas_call | solution.py:670

commit v3 on v2

--- a/solution.py
+++ b/solution.py
@@ -16,6 +16,9 @@
 BF16 = jnp.bfloat16
 MESH = pl.DeviceIdType.MESH
 DIRS = ((-1, -1), (-1, 0), (-1, 1), (0, -1), (0, 1), (1, -1), (1, 0), (1, 1))
+
+SIDES = (3, 4, 0, 2, 5, 7)
+ENDS = (1, 6)
 
 
 def split(value):
@@ -88,6 +91,8 @@
     osem,
     field,
     spread,
+    e_high,
+    e_low,
 ):
     N, W, ES, OV, CS, COLS, MODES, KR = cfg
     H = OV + 1
@@ -201,7 +206,7 @@
             elif da == 0:
                 part, dst = cs.at[(db + 1) // 2], cc.at[(1 - db) // 2]
             else:
-                part = src.at[rows, pl.ds(ES - SUB if db > 0 else 0, SUB)]
+                part = cs.at[(db + 1) // 2, pl.ds(0, H), pl.ds(ES - SUB if da > 0 else 0, SUB)]
                 dst = kk.at[(1 - da) + (1 - db) // 2]
             copies.append(
                 pltpu.make_async_remote_copy(
@@ -224,8 +229,8 @@
 
         lax.fori_loop(0, ES, body, 0)
 
-    def send_strips(copies):
-        for d in (3, 4, 1, 6, 0, 2, 5, 7):
+    def send_strips(copies, dirs):
+        for d in dirs:
 
             @pl.when(valid(d))
             def _():
@@ -263,8 +268,12 @@
         for side, top in ((0, 0), (1, CS + H)):
             for j in range(H):
                 dst[top + j, SUB + OV : SUB + OV + CS, :] = rr[side, j, own, :]
-                dst[top + j, left : left + H, :] = kk[2 * side, j, base : base + H, :]
-                dst[top + j, right : right + H, :] = kk[2 * side + 1, j, lo : lo + H, :]
+                row = (lo if side else base) + j
+                for q in range(H):
+                    at = left + q
+                    dst[top + j, at : at + 1, :] = kk[2 * side, q, row : row + 1, :]
+                    at = right + q
+                    dst[top + j, at : at + 1, :] = kk[2 * side + 1, q, row : row + 1, :]
 
     def coarse_copy(slot, k, ref):
         _, target = other(k)
@@ -334,7 +343,7 @@
     first = strips(0, x0, row0, col0, cs0, cor0)
     pack(x0, cs0)
     pl.semaphore_wait(barrier, count)
-    send_strips(first)
+    send_strips(first, SIDES + ENDS)
     d0[...] = jnp.zeros(d0.shape, F32)
     wdeep[...] = jnp.zeros(wdeep.shape, F32)
 
@@ -356,6 +365,13 @@
         return carry
 
     lax.fori_loop(0, LOCAL // step, left_side_perm, 0)
+    line = lax.broadcasted_iota(jnp.int32, (2 * H * ES, LOCAL), 0)
+    col = line >> int(math.log2(ES))
+    col = jnp.where(col < H, col + lo, col - H + hi)
+    pos = (line & (ES - 1)) * ES + col
+    edge = jnp.where(pos == numbering, 1.0, 0.0).astype(BF16)
+    e_high[...] = dot(edge, t_high[...]).astype(BF16)
+    e_low[...] = dot(edge, t_low[...]).astype(BF16)
     m_high, m_low = split(jnp.concatenate([basis, jnp.zeros((SUB - MODES, LOCAL), F32)], axis=0))
     bw[0] = dot(m_high, perm_t[...]).astype(BF16)
     bw[1] = dot(m_low, perm_t[...]).astype(BF16)
@@ -463,6 +479,10 @@
             for copy in writes:
                 copy.start()
         if it < ITERS:
+            value = dot3(e_high[...], e_low[...], x_high[...], x_low[...])
+            cs1[it] = value.reshape(2, H, ES, COLS)
+            copies = strips(it + 1, z.at[it], row1.at[it], col1.at[it], cs1.at[it], cor1.at[it])
+            send_strips(copies, SIDES)
 
             def solve(i, carry):
                 rows = pl.ds(pl.multiple_of(i * step, step), step)
@@ -471,9 +491,7 @@
                 return carry
 
             lax.fori_loop(0, LOCAL // step, solve, 0)
-            pack(z.at[it], cs1.at[it])
-            copies = strips(it + 1, z.at[it], row1.at[it], col1.at[it], cs1.at[it], cor1.at[it])
-            send_strips(copies)
+            send_strips(copies, ENDS)
             pending.append(copies)
         coarse_relay(it, ref)
         coarse_recv(it, ref)
@@ -640,6 +658,8 @@
         pltpu.SemaphoreType.DMA((4,)),
         pltpu.VMEM((LANES, LANES), F32),
         pltpu.VMEM((LANES, LOCAL), F32),
+        pltpu.VMEM((2 * H * ES, LOCAL), BF16),
+        pltpu.VMEM((2 * H * ES, LOCAL), BF16),
     ]
     out = jax.ShapeDtypeStruct((CS, ES, COLS), F32)
     anywhere = pl.BlockSpec(memory_space=pl.ANY)
@@ -651,7 +671,7 @@
         out_specs=(anywhere,) * 4 + (vmem,),
         scratch_shapes=scratch,
         compiler_params=pltpu.CompilerParams(
-            collective_id=0, has_side_effects=True, vmem_limit_bytes=60 * 2**20
+            collective_id=0, has_side_effects=True, vmem_limit_bytes=67043328
         ),
         name="schwarz",
     )(

time: 83.1 us -> 80.4 us (0.968)
  Pallas kernels: 82.2 us -> 79.5 us
    pallas_call x1, Pallas kernels: 78 us -> 75.4 us  [local(): pl.pallas_call(functools.partial(kernel, (N, W, ES, OV, CS, COLS, MODES,...]
where the time goes in v3:
time: 80.4 us; the launch traced here: 80.2 us
  Pallas kernels  79.5 us (99%)
    pallas_call x1, Pallas kernels, local(): pl.pallas_call(functools.partial(kernel, (N, W, ES, OV, CS, COLS, MODES,...  75.4 us
    pallas_call x1, Pallas kernels, local(): pl.pallas_call(functools.partial(finish, OV, CS), grid=(CS // block,), ou...  4.15 us

profile of v3, /device:TPU:1, one launch (start us, length us, event | category | flops | bytes accessed | tf_op | source)
XLA Modules:
  0.0 80.2 jit_solution(14348566113709105034)
XLA Ops:
  0.6 75.4 %schwarz.1 = (f32[28,32,256]{2,1,0:T(8,128)}, f32[28,32,256]{2,1,0:T(8,128)}, f32[28,32,256]{2,1,0:T(8,128)}, f32[28,32,256]{2,1,0:T(8,128)}, f32[8,256]{1,0:T(8,128)}) custom-call(f32[28,28,256]{2,1,0:T(8,128)} %rhs_ref.1, f32[28,28,256]{2,1,0:T(8,128)} %guess_ref.1, s32[28,28]{1,0:T(8,128)} %map_ref.1, f32[8]{0:T(128)} %class_ref.1, s32[1,1024]{1,0:T(1,128)} %bitcast.3, ...), custom_call_target="tpu_custom_call" | custom-call | tf_op jit(solution)/shard_map/schwarz/pallas_call | solution.py:667
  76.0 4.2 %finish.1 = (f32[28,28,256]{2,1,0:T(8,128)}, f32[28,28,256]{2,1,0:T(8,128)}) custom-call(f32[28,32,256]{2,1,0:T(8,128)} %get-tuple-element.7.sol, f32[28,32,256]{2,1,0:T(8,128)} %get-tuple-element.8.direction, f32[28,32,256]{2,1,0:T(8,128)} %get-tuple-element.9.res, f32[28,32,256]{2,1,0:T(8,128)} %get-tuple-element.10.image, f32[8,256]{1,0:T(8,128)} %get-tuple-element.11.size), custom_call_target="tpu_custom_call" | custom-call | tf_op jit(solution)/shard_map/finish/pallas_call | solution.py:690

commit v4 on v3

--- a/solution.py
+++ b/solution.py
@@ -250,10 +250,17 @@
             def _():
                 copies[d].wait_send()
 
-    def unpack(dst, src, rr, cc, kk):
-        def centre(i, carry):
+    def centre(dst, src):
+        def body(i, carry):
             u = OV + i
             dst[u + 1, SUB : SUB + ES, :] = src[u]
+            return carry
+
+        lax.fori_loop(0, CS, body, 0)
+
+    def unpack(dst, rr, cc, kk):
+        def sides(i, carry):
+            u = OV + i
             for j in range(H):
                 p = SUB - 1 + j
                 dst[u + 1, p : p + 1, :] = cc[0, j, pl.ds(u, 1), :]
@@ -261,7 +268,7 @@
                 dst[u + 1, p : p + 1, :] = cc[1, j, pl.ds(u, 1), :]
             return carry
 
-        lax.fori_loop(0, CS, centre, 0)
+        lax.fori_loop(0, CS, sides, 0)
         own = slice(OV, OV + CS)
         left, right = SUB - 1, SUB + CS + OV
         base = hi - (ES - SUB)
@@ -376,8 +383,15 @@
     bw[0] = dot(m_high, perm_t[...]).astype(BF16)
     bw[1] = dot(m_low, perm_t[...]).astype(BF16)
 
+    centre(d0, x0)
+
+    def start_sol(i, carry):
+        sol[i] = x0[OV + i, :, 0:COLS]
+        return carry
+
+    lax.fori_loop(0, CS, start_sol, 0)
     recv_strips(first)
-    unpack(d0, x0, row0, col0, cor0)
+    unpack(d0, row0, col0, cor0)
 
     def modes(u, carry):
         value = d0[u, :, 2 * COLS :]
@@ -437,12 +451,6 @@
         return carry
 
     lax.fori_loop(0, ES, first_residual, 0)
-
-    def start_sol(i, carry):
-        sol[i] = d0[OV + i + 1, SUB : SUB + ES, 0:COLS]
-        return carry
-
-    lax.fori_loop(0, CS, start_sol, 0)
 
     def coarse_rows():
         return dot3(bw[0], bw[1], x_high[...], x_low[...])
@@ -492,6 +500,7 @@
 
             lax.fori_loop(0, LOCAL // step, solve, 0)
             send_strips(copies, ENDS)
+            centre(wdeep, z.at[it])
             pending.append(copies)
         coarse_relay(it, ref)
         coarse_recv(it, ref)
@@ -532,9 +541,6 @@
             break
         g_high, g_low = split(ref[:, :, 0:SUB, :].reshape(N * W * SUB, COLS))
         s_high, s_low = split(dot3(kmat[0], kmat[1], g_high, g_low))
-        recv_strips(copies)
-        unpack(wdeep, z.at[it], row1.at[it], col1.at[it], cor1.at[it])
-
         if it > 0:
 
             def advance(i, carry):
@@ -544,6 +550,8 @@
                 return carry
 
             lax.fori_loop(0, CS, advance, 0)
+        recv_strips(copies)
+        unpack(wdeep, row1.at[it], col1.at[it], cor1.at[it])
         chunk = DH // 2
 
         def coarse_part(i, carry):

time: 80.4 us -> 79.7 us (level)
  no operation moved by 1% of the time
where the time goes in v4:
time: 79.7 us; the launch traced here: 79.5 us
  Pallas kernels  78.8 us (99%)
    pallas_call x1, Pallas kernels, local(): pl.pallas_call(functools.partial(kernel, (N, W, ES, OV, CS, COLS, MODES,...  74.7 us
    pallas_call x1, Pallas kernels, local(): pl.pallas_call(functools.partial(finish, OV, CS), grid=(CS // block,), ou...  4.15 us

profile of v4, /device:TPU:1, one launch (start us, length us, event | category | flops | bytes accessed | tf_op | source)
XLA Modules:
  0.0 79.5 jit_solution(15336388003700147197)
XLA Ops:
  0.6 74.7 %schwarz.1 = (f32[28,32,256]{2,1,0:T(8,128)}, f32[28,32,256]{2,1,0:T(8,128)}, f32[28,32,256]{2,1,0:T(8,128)}, f32[28,32,256]{2,1,0:T(8,128)}, f32[8,256]{1,0:T(8,128)}) custom-call(f32[28,28,256]{2,1,0:T(8,128)} %rhs_ref.1, f32[28,28,256]{2,1,0:T(8,128)} %guess_ref.1, s32[28,28]{1,0:T(8,128)} %map_ref.1, f32[8]{0:T(128)} %class_ref.1, s32[1,1024]{1,0:T(1,128)} %bitcast.3, ...), custom_call_target="tpu_custom_call" | custom-call | tf_op jit(solution)/shard_map/schwarz/pallas_call | solution.py:675
  75.3 4.2 %finish.1 = (f32[28,28,256]{2,1,0:T(8,128)}, f32[28,28,256]{2,1,0:T(8,128)}) custom-call(f32[28,32,256]{2,1,0:T(8,128)} %get-tuple-element.7.sol, f32[28,32,256]{2,1,0:T(8,128)} %get-tuple-element.8.direction, f32[28,32,256]{2,1,0:T(8,128)} %get-tuple-element.9.res, f32[28,32,256]{2,1,0:T(8,128)} %get-tuple-element.10.image, f32[8,256]{1,0:T(8,128)} %get-tuple-element.11.size), custom_call_target="tpu_custom_call" | custom-call | tf_op jit(solution)/shard_map/finish/pallas_call | solution.py:698
